TPU v7x, 32 devices: a whole 2x2x4 slice. The times are simulated.
32 devices in a mesh: row: 8 (over y, x, core), col: 4 (over z).
Axes of the slice: x: 2, y: 2, z: 4, core: 2. Of those that a mesh axis runs over, the one named last changes fastest.
Arguments:
- cotangent: bfloat16 [256, 256, 128], P('row', 'col'), may hold values from -6 to 6
- activations: bfloat16 [3, 256, 256, 128], P(None, 'row', 'col'), may hold values from 0 to 2
- active_masks: int32 [3, 256, 256, 128], P(None, 'row', 'col'), may hold values 0 or 1
- weights: bfloat16 [3, 9, 128, 128], replicated, may hold values from -0.1875 to 0.1875
Outputs:
- data_gradient: bfloat16 [256, 256, 128], P('row', 'col')
- weight_gradients: float32 [3, 9, 128, 128], replicated
All inputs are finite; a program needn't handle non-finite values. No bound on the sum of `active_masks` on one device may be relied on, other than what follows from the above.
Results may differ from a plain program's by a relative error of at most 0.0054.
Values may be sent and summed in bfloat16 or wider, within the bound.
A program may use at most 64 MiB of HBM per device.

v0:
```python
import jax
import jax.numpy as jnp
from jax import lax
from jax.sharding import PartitionSpec as P


def extended(block, sides, width):
    for axis, dim in sides:
        count = lax.axis_size(axis)
        forward = [(i, i + 1) for i in range(count - 1)]
        backward = [(target, source) for source, target in forward]
        low = lax.ppermute(
            lax.slice_in_dim(block, block.shape[dim] - width, None, axis=dim), axis, forward
        )
        high = lax.ppermute(lax.slice_in_dim(block, 0, width, axis=dim), axis, backward)
        block = jnp.concatenate([low, block, high], axis=dim)
    return block


def tap_columns(padded, height, extent, dilation):
    pieces = []
    for tap_down in range(3):
        for tap_across in range(3):
            start_down = dilation * (2 - tap_down)
            start_across = dilation * (2 - tap_across)
            pieces.append(
                padded[start_down : start_down + height, start_across : start_across + extent]
            )
    return jnp.stack(pieces, axis=2)


def mirrored(local_tile):
    stripe = lax.all_to_all(local_tile, "col", split_axis=0, concat_axis=1, tiled=True)
    arrived = lax.all_to_all(stripe, ("row", "col"), split_axis=1, concat_axis=0, tiled=True)
    flipped = jnp.transpose(arrived, (1, 0, 2))
    return lax.all_to_all(flipped, "col", split_axis=1, concat_axis=0, tiled=True)


def per_device(cotangent, activations, active_masks, weights):
    height, extent, channels = cotangent.shape
    map_side = height * lax.axis_size("row")
    layers = weights.shape[0]
    gradient = cotangent
    collected = []
    for layer_index in reversed(range(layers)):
        dilation = 2**layer_index
        mask_now = active_masks[layer_index] > 0
        inputs_now = jnp.where(
            mask_now, activations[layer_index], jnp.zeros_like(activations[layer_index])
        )
        mirror = mirrored(gradient)
        symmetric = ((gradient.astype(jnp.float32) + mirror.astype(jnp.float32)) * 0.5).astype(
            jnp.bfloat16
        )
        padded = extended(symmetric, (("row", 0), ("col", 1)), dilation)
        stacked = tap_columns(padded, height, extent, dilation)
        partial_value = (
            jnp.einsum("yxi,yxko->kio", inputs_now, stacked, preferred_element_type=jnp.float32)
            / map_side
        )
        input_change = jnp.einsum(
            "yxko,kio->yxi", stacked, weights[layer_index], preferred_element_type=jnp.float32
        )
        gradient = (
            gradient.astype(jnp.float32) + jnp.where(mask_now, input_change, jnp.float32(0.0))
        ).astype(jnp.bfloat16)
        collected.append(lax.psum(partial_value, ("row", "col")))
    kernel_stack = jnp.stack(collected[::-1])
    return (gradient, kernel_stack)


def solution(mesh):
    in_specs = (
        P("row", "col", None),
        P(None, "row", "col", None),
        P(None, "row", "col", None),
        P(),
    )
    out_specs = (P("row", "col", None), P())
    return jax.shard_map(
        per_device, mesh=mesh, in_specs=in_specs, out_specs=out_specs, check_vma=False
    )
```

profile of v0, /device:TPU:0, one launch (start us, length us, event | category | flops | bytes accessed | tf_op | source)
XLA Modules:
  0.0 377.1 jit_solution(14077130573089412062)
XLA Ops:
  7.2 20.8 %all_to_all.135 = bf16[32,64,128]{2,1,0:T(8,128)(2,1)S(1)} all-to-all(bf16[32,64,128]{2,1,0:T(8,128)(2,1)} %param.4), channel_id=1, replica_groups=mesh['row'=8,'col'=4] {'col'}, dimensions={0} | all-to-all | bytes 1048576 | tf_op jit(solution)/shard_map/all_to_all | solution.py:33
  28.5 17.8 %all_to_all.136 = bf16[8,256,128]{2,0,1:T(8,128)(2,1)S(1)} all-to-all(bf16[8,256,128]{2,0,1:T(8,128)(2,1)S(1)} %copy.84), channel_id=1, replica_groups=mesh['row'=8,'col'=4] {'row','col'}, dimensions={1} | all-to-all | bytes 1048576 | tf_op jit(solution)/shard_map/all_to_all | solution.py:34
  46.3 18.6 %all_to_all.137 = bf16[8,256,128]{2,0,1:T(8,128)(2,1)S(1)} all-to-all(bf16[8,256,128]{2,0,1:T(8,128)(2,1)S(1)} %bitcast.279), channel_id=1, replica_groups=mesh['row'=8,'col'=4] {'col'}, dimensions={1} | all-to-all | bytes 1048576 | tf_op jit(solution)/shard_map/all_to_all | solution.py:36
  68.0 3.5 collective-permute-done.1
  71.6 2.1 collective-permute-start.3
  75.5 4.1 %collective-permute-done.2 = bf16[40,4,128]{2,1,0:T(4,128)(2,1)S(1)} collective-permute-done((bf16[40,4,128]{2,1,0:T(4,128)(2,1)S(1)}, bf16[40,4,128]{2,1,0:T(4,128)(2,1)S(1)}, u32[]{:S(2)}, u32[]{:S(2)}) %collective-permute-start.2) | collective-permute-done | bytes 40992 | tf_op jit(solution)/shard_map/ppermute | solution.py:15
  82.7 18.5 %all_to_all.138 = bf16[32,64,128]{2,1,0:T(8,128)(2,1)S(1)} all-to-all(bf16[32,64,128]{2,1,0:T(8,128)(2,1)S(1)} %fusion.3), channel_id=1, replica_groups=mesh['row'=8,'col'=4] {'col'}, dimensions={0} | all-to-all | bytes 1048576 | tf_op jit(solution)/shard_map/all_to_all | solution.py:33
  101.6 18.2 %all_to_all.139 = bf16[8,256,128]{2,0,1:T(8,128)(2,1)S(1)} all-to-all(bf16[8,256,128]{2,0,1:T(8,128)(2,1)S(1)} %copy.98), channel_id=1, replica_groups=mesh['row'=8,'col'=4] {'row','col'}, dimensions={1} | all-to-all | bytes 1048576 | tf_op jit(solution)/shard_map/all_to_all | solution.py:34
  119.9 18.6 %all_to_all.140 = bf16[8,256,128]{2,0,1:T(8,128)(2,1)S(1)} all-to-all(bf16[8,256,128]{2,0,1:T(8,128)(2,1)S(1)} %bitcast.282), channel_id=1, replica_groups=mesh['row'=8,'col'=4] {'col'}, dimensions={1} | all-to-all | bytes 1048576 | tf_op jit(solution)/shard_map/all_to_all | solution.py:36
  141.6 3.5 collective-permute-done.5
  145.1 2.1 collective-permute-start.7
  148.7 4.2 %collective-permute-done.6 = bf16[36,2,128]{2,1,0:T(2,128)(2,1)S(1)} collective-permute-done((bf16[36,2,128]{2,1,0:T(2,128)(2,1)S(1)}, bf16[36,2,128]{2,1,0:T(2,128)(2,1)S(1)}, u32[]{:S(2)}, u32[]{:S(2)}) %collective-permute-start.6) | collective-permute-done | bytes 18464 | tf_op jit(solution)/shard_map/ppermute | solution.py:15
  155.8 18.8 %all_to_all.141 = bf16[32,64,128]{2,1,0:T(8,128)(2,1)S(1)} all-to-all(bf16[32,64,128]{2,1,0:T(8,128)(2,1)S(1)} %fusion.4), channel_id=1, replica_groups=mesh['row'=8,'col'=4] {'col'}, dimensions={0} | all-to-all | bytes 1048576 | tf_op jit(solution)/shard_map/all_to_all | solution.py:33
  175.0 17.7 %all_to_all.142 = bf16[8,256,128]{2,0,1:T(8,128)(2,1)S(1)} all-to-all(bf16[8,256,128]{2,0,1:T(8,128)(2,1)S(1)} %copy.104), channel_id=1, replica_groups=mesh['row'=8,'col'=4] {'row','col'}, dimensions={1} | all-to-all | bytes 1048576 | tf_op jit(solution)/shard_map/all_to_all | solution.py:34
  192.8 18.6 %all_to_all.143 = bf16[8,256,128]{2,0,1:T(8,128)(2,1)S(1)} all-to-all(bf16[8,256,128]{2,0,1:T(8,128)(2,1)S(1)} %bitcast.285), channel_id=1, replica_groups=mesh['row'=8,'col'=4] {'col'}, dimensions={1} | all-to-all | bytes 1048576 | tf_op jit(solution)/shard_map/all_to_all | solution.py:36
  214.6 2.2 fusion.7
  218.0 2.1 collective-permute-start.11
  221.4 2.3 fusion.9
  223.7 2.1 collective-permute-done.10
  227.2 2.1 copy-done.2
  229.4 2.3 fusion.11
  231.6 4.5 %fusion.5 = bf16[32,64,128]{2,1,0:T(8,128)(2,1)} fusion(pred[32,64,128]{2,1,0:T(32,128)(4,1)S(1)} %get-tuple-element.16, bf16[32,64,9,128]{3,1,0,2:T(8,128)(2,1)} %copy-done.2, bf16[32,64,128]{2,1,0:T(8,128)(2,1)S(1)} %fusion.4, bf16[3,9,128,128]{3,2,1,0:T(8,128)(2,1)S(1)} %copy-done.4), kind=kOutput, calls=%fused_computation.15 | convolution fusion | flops 605028352 | bytes 6324224 | tf_op jit(solution)/shard_map/yxko,kio->yxi/dot_general | solution.py:61
  236.2 130.7 %all-reduce.3.cloned.1.call-done = (f32[1,9,128,128]{2,3,1,0:T(8,128)}, f32[1,9,128,128]{2,3,1,0:T(8,128)}, f32[1,9,128,128]{2,3,1,0:T(8,128)}) async-done(((f32[1,9,128,128]{2,3,1,0:T(8,128)}, f32[1,9,128,128]{2,3,1,0:T(8,128)}, f32[1,9,128,128]{2,3,1,0:T(8,128)}), (f32[1,9,128,128]{2,3,1,0:T(8,128)}, f32[1,9,128,128]{2,3,1,0:T(8,128)}, f32[1,9,128,128]{2,3,1,0:T(8,128)})) %all-reduce.3.cloned.1.call-update) | async-done | bytes 1769488 | tf_op jit(solution)/shard_map/psum | solution.py:67
  368.4 1.9 copy.109
  (85 shorter events, 25.1 us)
Async XLA Ops:
  7.2 359.7 %all-reduce.3.cloned.1.call-start = ((), (), s32[]{:S(2)}) async-start(), calls=%async_computation.9 | async-start | bytes 3538944 | tf_op jit(solution)/shard_map/psum | solution.py:67
  28.1 37.1 %copy-start.1 = (bf16[32,64,128]{2,1,0:T(8,128)(2,1)S(1)}, bf16[32,64,128]{2,1,0:T(8,128)(2,1)}, u32[]{:S(2)}) copy-start(bf16[32,64,128]{2,1,0:T(8,128)(2,1)} %param.4) | copy-start | bytes 1572868
  28.5 46.6 %copy-start = (s32[3,32,64,128]{3,2,1,0:T(8,128)S(1)}, s32[3,32,64,128]{3,2,1,0:T(8,128)}, u32[]{:S(2)}) copy-start(s32[3,32,64,128]{3,2,1,0:T(8,128)} %param.6) | copy-start | bytes 9437188
  65.4 2.6 collective-permute-start
  66.7 4.9 %collective-permute-start.1 = (bf16[4,64,128]{2,1,0:T(8,128)(2,1)S(1)}, bf16[4,64,128]{2,1,0:T(8,128)(2,1)S(1)}, u32[]{:S(2)}, u32[]{:S(2)}) collective-permute-start(bf16[4,64,128]{2,1,0:T(8,128)(2,1)S(1)} %get-tuple-element.35), channel_id=1, source_target_pairs={{4,0},{8,4},{12,8},{16,12},{20,16},{24,20},{28,24},{5,1},{9,5},{13... | collective-permute-start | bytes 196616 | tf_op jit(solution)/shard_map/ppermute | solution.py:15
  71.6 3.9 %collective-permute-start.3 = (bf16[40,4,128]{2,1,0:T(4,128)(2,1)S(1)}, bf16[40,4,128]{2,1,0:T(4,128)(2,1)S(1)}, u32[]{:S(2)}, u32[]{:S(2)}) collective-permute-start(bf16[40,4,128]{2,1,0:T(4,128)(2,1)S(1)} %get-tuple-element.20), channel_id=1, source_target_pairs={{0,1},{1,2},{2,3},{4,5},{5,6},{6,7},{8,9},{9,10},{10,11},{12,13},{... | collective-permute-start | bytes 122888 | tf_op jit(solution)/shard_map/ppermute | solution.py:12
  73.8 5.9 %collective-permute-start.2 = (bf16[40,4,128]{2,1,0:T(4,128)(2,1)S(1)}, bf16[40,4,128]{2,1,0:T(4,128)(2,1)S(1)}, u32[]{:S(2)}, u32[]{:S(2)}) collective-permute-start(bf16[40,4,128]{2,1,0:T(4,128)(2,1)S(1)} %get-tuple-element.21), channel_id=1, source_target_pairs={{1,0},{2,1},{3,2},{5,4},{6,5},{7,6},{9,8},{10,9},{11,10},{13,12},{... | collective-permute-start | bytes 122888 | tf_op jit(solution)/shard_map/ppermute | solution.py:15
  80.1 1.2 copy-start.4
  139.0 2.6 collective-permute-start.4
  140.3 4.8 %collective-permute-start.5 = (bf16[2,64,128]{2,1,0:T(8,128)(2,1)S(1)}, bf16[2,64,128]{2,1,0:T(8,128)(2,1)S(1)}, u32[]{:S(2)}, u32[]{:S(2)}) collective-permute-start(bf16[2,64,128]{2,1,0:T(8,128)(2,1)S(1)} %get-tuple-element.33), channel_id=1, source_target_pairs={{4,0},{8,4},{12,8},{16,12},{20,16},{24,20},{28,24},{5,1},{9,5},{13... | collective-permute-start | bytes 98312 | tf_op jit(solution)/shard_map/ppermute | solution.py:15
  145.1 3.6 collective-permute-start.7
  147.3 5.7 %collective-permute-start.6 = (bf16[36,2,128]{2,1,0:T(2,128)(2,1)S(1)}, bf16[36,2,128]{2,1,0:T(2,128)(2,1)S(1)}, u32[]{:S(2)}, u32[]{:S(2)}) collective-permute-start(bf16[36,2,128]{2,1,0:T(2,128)(2,1)S(1)} %get-tuple-element.25), channel_id=1, source_target_pairs={{1,0},{2,1},{3,2},{5,4},{6,5},{7,6},{9,8},{10,9},{11,10},{13,12},{... | collective-permute-start | bytes 55304 | tf_op jit(solution)/shard_map/ppermute | solution.py:15
  175.0 39.6 %copy-start.3 = (bf16[3,32,64,128]{3,2,1,0:T(8,128)(2,1)S(1)}, bf16[3,32,64,128]{3,2,1,0:T(8,128)(2,1)}, u32[]{:S(2)}) copy-start(bf16[3,32,64,128]{3,2,1,0:T(8,128)(2,1)} %param.5) | copy-start | bytes 4718596
  211.8 5.0 %collective-permute-start.8 = (bf16[1,64,128]{2,1,0:T(8,128)(2,1)S(1)}, bf16[1,64,128]{2,1,0:T(8,128)(2,1)S(1)}, u32[]{:S(2)}, u32[]{:S(2)}) collective-permute-start(bf16[1,64,128]{2,1,0:T(8,128)(2,1)S(1)} %get-tuple-element.30), channel_id=1, source_target_pairs={{0,4},{4,8},{8,12},{12,16},{16,20},{20,24},{24,28},{1,5},{5,9},{9,... | collective-permute-start | bytes 49160 | tf_op jit(solution)/shard_map/ppermute | solution.py:12
  213.1 4.8 %collective-permute-start.9 = (bf16[1,64,128]{2,1,0:T(8,128)(2,1)S(1)}, bf16[1,64,128]{2,1,0:T(8,128)(2,1)S(1)}, u32[]{:S(2)}, u32[]{:S(2)}) collective-permute-start(bf16[1,64,128]{2,1,0:T(8,128)(2,1)S(1)} %get-tuple-element.31), channel_id=1, source_target_pairs={{4,0},{8,4},{12,8},{16,12},{20,16},{24,20},{28,24},{5,1},{9,5},{13... | collective-permute-start | bytes 49160 | tf_op jit(solution)/shard_map/ppermute | solution.py:15
  218.0 5.7 %collective-permute-start.11 = (bf16[34,1,128]{2,1,0:T(2,128)(2,1)S(1)}, bf16[34,1,128]{2,1,0:T(2,128)(2,1)S(1)}, u32[]{:S(2)}, u32[]{:S(2)}) collective-permute-start(bf16[34,1,128]{2,1,0:T(2,128)(2,1)S(1)} %get-tuple-element.28), channel_id=1, source_target_pairs={{0,1},{1,2},{2,3},{4,5},{5,6},{6,7},{8,9},{9,10},{10,11},{12,13},{... | collective-permute-start | bytes 26120 | tf_op jit(solution)/shard_map/ppermute | solution.py:12
  220.1 5.6 %collective-permute-start.10 = (bf16[34,1,128]{2,1,0:T(2,128)(2,1)S(1)}, bf16[34,1,128]{2,1,0:T(2,128)(2,1)S(1)}, u32[]{:S(2)}, u32[]{:S(2)}) collective-permute-start(bf16[34,1,128]{2,1,0:T(2,128)(2,1)S(1)} %get-tuple-element.29), channel_id=1, source_target_pairs={{1,0},{2,1},{3,2},{5,4},{6,5},{7,6},{9,8},{10,9},{11,10},{13,12},{... | collective-permute-start | bytes 26120 | tf_op jit(solution)/shard_map/ppermute | solution.py:15
  227.2 2.1 copy-start.2
Sparse Core Ops, SparseCore 0:
  231.8 135.0 all-reduce.2
where the time goes:
time: 378 us; the launch traced here: 377 us
  blocking collectives  168 us (44%)
  waiting for transfers between devices  149 us (39%)
  starting transfers between devices  18.2 us (5%)
  between operations  14.6 us (4%)
  matrix products  14.2 us (4%)
  local copies, waits for them, and re-layouts  8.85 us (2%)
  other arithmetic  4.35 us (1%)
    psum x1, waiting for transfers between devices, per_device(): collected.append(lax.psum(partial_value, ('row', 'col')))  131 us
    all_to_all x3, blocking collectives, mirrored(): lax.all_to_all(local_tile, 'col', split_axis=0, concat_axis=1, tiled=True)  58.2 us
    all_to_all x3, blocking collectives, mirrored(): lax.all_to_all(flipped, 'col', split_axis=1, concat_axis=0, tiled=True)  55.8 us
    all_to_all x3, blocking collectives, mirrored(): lax.all_to_all(stripe, ('row', 'col'), split_axis=1, concat_axis=0, tiled...  53.6 us
    ppermute x6, waiting for transfers between devices, extended(): lax.ppermute(lax.slice_in_dim(block, 0, width, axis=dim), axis, backward)  18.5 us
    ppermute x6, starting transfers between devices, extended(): lax.ppermute(lax.slice_in_dim(block, block.shape[dim] - width, None, axis...  10.2 us
    ppermute x6, starting transfers between devices, extended(): lax.ppermute(lax.slice_in_dim(block, 0, width, axis=dim), axis, backward)  7.93 us
  transfers between devices with their start and end apart: 13, of which 8 were waited for; matrix products, arithmetic and copies ran while one was open for 3% of the time, Pallas kernels for 0%

commit v1 on v0

v1 whole, which is shorter than its diff:
```python
import functools

import jax
import jax.numpy as jnp
from jax import lax
from jax.experimental import pallas as pl
from jax.experimental.pallas import tpu as pltpu
from jax.sharding import PartitionSpec as P

MESH = pl.DeviceIdType.MESH
VMEM = pl.BlockSpec(memory_space=pltpu.VMEM)
LATE = True


def remote(src, dst, send, recv, row, col):
    return pltpu.make_async_remote_copy(
        src_ref=src,
        dst_ref=dst,
        send_sem=send,
        recv_sem=recv,
        device_id=(row, col),
        device_id_type=MESH,
    )


def exchange_kernel(chips, cols, g, arrived, relay, send_a, recv_a, send_b, recv_b):
    row, col = lax.axis_index("row"), lax.axis_index("col")
    chip, core = lax.div(row, 2), lax.rem(row, 2)
    height, extent, _ = g.shape
    half = extent // 2
    part = height // chips
    barrier = pltpu.get_barrier_semaphore()

    def first_target(b):
        return (2 * b + core, chip) if LATE else (2 * b + core, col)

    def first_source(k):
        return (2 * col + core, k) if LATE else (2 * k + core, col)

    def second_target(k, h):
        return (2 * k + h, col) if LATE else (2 * col + h, k)

    def second_source(b, h):
        return (2 * b + h, col) if LATE else (2 * b + h, chip)

    def other(place):
        return jnp.logical_or(place[0] != row, place[1] != col)

    def signal(place):
        @pl.when(other(place))
        def _():
            pl.semaphore_signal(barrier, inc=1, device_id=place, device_id_type=MESH)

    for k in range(chips):
        signal(first_source(k))
        for h in range(2):
            signal(second_source(k, h))
    expected = jnp.int32(0)
    for k in range(chips):
        expected += other(first_target(k)).astype(jnp.int32)
        for h in range(2):
            expected += other(second_target(k, h)).astype(jnp.int32)
    pl.semaphore_wait(barrier, expected)

    slot = col if LATE else chip

    def first(b):
        place = first_target(b)
        src = g.at[pl.ds(b * part, part)]
        return place, src, relay.at[slot], send_a.at[b], recv_a.at[slot]

    def second(k, h):
        place = second_target(k, h)
        src = relay.at[k, :, pl.ds(h * half, half)]
        dst = arrived.at[pl.ds(core * height + chip * part, part)]
        return place, src, dst, send_b.at[2 * k + h], recv_b.at[row]

    def begin(item):
        place, src, dst, send, recv = item
        away = other(place)

        @pl.when(away)
        def _():
            remote(src, dst, send, recv, *place).start()

        @pl.when(jnp.logical_not(away))
        def _():
            pltpu.make_async_copy(src, dst, recv).start()

    def finish(item):
        place, src, dst, send, recv = item

        @pl.when(other(place))
        def _():
            remote(src, dst, send, recv, *place).wait_send()

    for b in range(chips):
        begin(first(b))
    for k in range(chips):
        pltpu.make_async_copy(relay.at[k], relay.at[k], recv_a.at[k]).wait()
        for h in range(2):
            begin(second(k, h))
    for b in range(chips):
        finish(first(b))
        for h in range(2):
            finish(second(b, h))
    for b in range(chips):
        for h in range(2):
            dst = arrived.at[pl.ds(h * height + b * part, part)]
            pltpu.make_async_copy(dst, dst, recv_b.at[2 * b + h]).wait()


def exchanged(gradient, index):
    height, extent, channels = gradient.shape
    rows, cols = lax.axis_size("row"), lax.axis_size("col")
    chips = rows // 2
    return pl.pallas_call(
        functools.partial(exchange_kernel, chips, cols),
        out_shape=jax.ShapeDtypeStruct((extent, height, channels), gradient.dtype),
        in_specs=[VMEM],
        out_specs=VMEM,
        scratch_shapes=[
            pltpu.VMEM((chips, height // chips, extent, channels), gradient.dtype),
            pltpu.SemaphoreType.DMA((chips,)),
            pltpu.SemaphoreType.DMA((chips,)),
            pltpu.SemaphoreType.DMA((rows,)),
            pltpu.SemaphoreType.DMA((rows,)),
        ],
        compiler_params=pltpu.CompilerParams(
            collective_id=index, has_side_effects=True
        ),
    )(gradient)


SIDES = [(-1, -1), (-1, 0), (-1, 1), (0, -1), (0, 1), (1, -1), (1, 0), (1, 1)]


def halo_kernel(rows, cols, *refs):
    sources, targets, (send, recv) = refs[:8], refs[8:16], refs[16:]
    row, col = lax.axis_index("row"), lax.axis_index("col")
    barrier = pltpu.get_barrier_semaphore()

    def there(step):
        down, across = row + step[0], col + step[1]
        inside = jnp.logical_and(
            jnp.logical_and(down >= 0, down < rows),
            jnp.logical_and(across >= 0, across < cols),
        )
        return inside, down, across

    expected = jnp.int32(0)
    for step in SIDES:
        inside, down, across = there(step)
        expected += inside.astype(jnp.int32)

        @pl.when(inside)
        def _():
            pl.semaphore_signal(
                barrier, inc=1, device_id=(down, across), device_id_type=MESH
            )

    pl.semaphore_wait(barrier, expected)
    for n, step in enumerate(SIDES):
        inside, down, across = there(step)

        @pl.when(inside)
        def _():
            remote(sources[n], targets[7 - n], send.at[n], recv.at[7 - n], down, across).start()

        @pl.when(jnp.logical_not(inside))
        def _():
            targets[n][...] = jnp.zeros_like(targets[n])

    for n, step in enumerate(SIDES):
        inside, down, across = there(step)

        @pl.when(inside)
        def _():
            remote(sources[n], targets[n], send.at[n], recv.at[n], down, across).wait()


def padded_symmetric(symmetric, d, index):
    height, extent, _ = symmetric.shape
    low, high = slice(0, d), slice(-d, None)
    down = {-1: low, 0: slice(None), 1: high}
    pieces = []
    for y, x in SIDES:
        piece = symmetric[down[y], down[x]]
        pieces.append(jnp.transpose(piece, (1, 0, 2)) if y == 0 else piece)
    got = pl.pallas_call(
        functools.partial(halo_kernel, lax.axis_size("row"), lax.axis_size("col")),
        out_shape=[jax.ShapeDtypeStruct(p.shape, p.dtype) for p in pieces],
        in_specs=[VMEM] * 8,
        out_specs=[VMEM] * 8,
        scratch_shapes=[pltpu.SemaphoreType.DMA((8,)), pltpu.SemaphoreType.DMA((8,))],
        compiler_params=pltpu.CompilerParams(
            collective_id=index, has_side_effects=True
        ),
    )(*pieces)
    left = jnp.transpose(got[3], (1, 0, 2))
    right = jnp.transpose(got[4], (1, 0, 2))
    top = jnp.concatenate([got[0], got[1], got[2]], axis=1)
    middle = jnp.concatenate([left, symmetric, right], axis=1)
    bottom = jnp.concatenate([got[5], got[6], got[7]], axis=1)
    return jnp.concatenate([top, middle, bottom], axis=0)


def reduce_kernel(
    layers, chips, cols, x, out, r1, s1, r2, s2, r3, send1, recv1, send2, recv2, send3, recv3,
    send4, recv4, send5, recv5, send6, recv6,
):
    row, col = lax.axis_index("row"), lax.axis_index("col")
    chip, core = lax.div(row, 2), lax.rem(row, 2)
    sibling = 2 * chip + 1 - core
    wide = jnp.float32

    def chip_at(j):
        return lax.rem(chip + j, chips)

    def col_at(j):
        return lax.rem(col + j, cols)

    barrier = pltpu.get_barrier_semaphore()
    pl.semaphore_signal(barrier, inc=1, device_id=(sibling, col), device_id_type=MESH)
    for j in range(1, chips):
        pl.semaphore_signal(
            barrier, inc=1, device_id=(2 * chip_at(j) + core, col), device_id_type=MESH
        )
    for j in range(1, cols):
        pl.semaphore_signal(barrier, inc=1, device_id=(row, col_at(j)), device_id_type=MESH)
    pl.semaphore_wait(barrier, chips + cols - 1)

    def p1(l):
        return remote(x.at[l, 1 - core], r1.at[l], send1.at[l], recv1.at[l], sibling, col)

    def p2(l, j):
        k = chip_at(j)
        return remote(s1.at[l, k], r2.at[l, j], send2.at[l, j], recv2.at[l, j], 2 * k + core, col)

    def p3(l, j):
        k = col_at(j)
        return remote(s2.at[l, k], r3.at[l, j], send3.at[l, j], recv3.at[l, j], row, k)

    def p4(l, j):
        mine = out.at[l, core, chip, col]
        return remote(mine, mine, send4.at[l, j], recv4.at[l, j], row, col_at(j))

    def p5(l, j):
        mine = out.at[l, core, chip]
        return remote(mine, mine, send5.at[l, j], recv5.at[l, j], 2 * chip_at(j) + core, col)

    def p6(l):
        mine = out.at[l, core]
        return remote(mine, mine, send6.at[l], recv6.at[l], sibling, col)

    for l in range(layers):
        p1(l).start()
    for l in range(layers):
        p1(l).wait_recv()
        s1[l] = (x[l, core].astype(wide) + r1[l].astype(wide)).astype(s1.dtype)
        for j in range(1, chips):
            p2(l, j).start()
    for l in range(layers):
        total = s1[l, chip].astype(wide)
        for j in range(1, chips):
            p2(l, j).wait_recv()
            total += r2[l, j].astype(wide)
        s2[l] = total.astype(s2.dtype)
        for j in range(1, cols):
            p3(l, j).start()
    for l in range(layers):
        total = s2[l, col].astype(wide)
        for j in range(1, cols):
            p3(l, j).wait_recv()
            total += r3[l, j].astype(wide)
        out[l, core, chip, col] = total.astype(out.dtype)
        for j in range(1, cols):
            p4(l, j).start()
    for l in range(layers):
        for j in range(1, cols):
            p4(l, j).wait_recv()
        for j in range(1, chips):
            p5(l, j).start()
    for l in range(layers):
        for j in range(1, chips):
            p5(l, j).wait_recv()
        p6(l).start()
    for l in range(layers):
        p6(l).wait_recv()
        p1(l).wait_send()
        p6(l).wait_send()
        for j in range(1, chips):
            p2(l, j).wait_send()
            p5(l, j).wait_send()
        for j in range(1, cols):
            p3(l, j).wait_send()
            p4(l, j).wait_send()


def reduced(partial, index):
    layers, taps, channels, lanes = partial.shape
    chips, cols = lax.axis_size("row") // 2, lax.axis_size("col")
    count = taps * channels // (2 * chips * cols)
    kind = jnp.bfloat16
    x = partial.astype(kind).reshape(layers, 2, chips, cols, count, lanes)
    dma = pltpu.SemaphoreType.DMA
    out = pl.pallas_call(
        functools.partial(reduce_kernel, layers, chips, cols),
        out_shape=jax.ShapeDtypeStruct(x.shape, kind),
        in_specs=[VMEM],
        out_specs=VMEM,
        scratch_shapes=[
            pltpu.VMEM((layers, chips, cols, count, lanes), kind),
            pltpu.VMEM((layers, chips, cols, count, lanes), kind),
            pltpu.VMEM((layers, chips, cols, count, lanes), kind),
            pltpu.VMEM((layers, cols, count, lanes), kind),
            pltpu.VMEM((layers, cols, count, lanes), kind),
            dma((layers,)), dma((layers,)),
            dma((layers, chips)), dma((layers, chips)),
            dma((layers, cols)), dma((layers, cols)),
            dma((layers, cols)), dma((layers, cols)),
            dma((layers, chips)), dma((layers, chips)),
            dma((layers,)), dma((layers,)),
        ],
        compiler_params=pltpu.CompilerParams(
            collective_id=index, has_side_effects=True
        ),
    )(x)
    return out.reshape(layers, taps, channels, lanes).astype(jnp.float32)


def tap_columns(padded, height, extent, dilation):
    pieces = []
    for tap_down in range(3):
        for tap_across in range(3):
            start_down = dilation * (2 - tap_down)
            start_across = dilation * (2 - tap_across)
            pieces.append(
                padded[start_down : start_down + height, start_across : start_across + extent]
            )
    return jnp.stack(pieces, axis=2)


def per_device(cotangent, activations, active_masks, weights):
    height, extent, channels = cotangent.shape
    map_side = height * lax.axis_size("row")
    layers = weights.shape[0]
    gradient = cotangent
    collected = []
    for layer_index in reversed(range(layers)):
        dilation = 2**layer_index
        mask_now = active_masks[layer_index] > 0
        inputs_now = jnp.where(
            mask_now, activations[layer_index], jnp.zeros_like(activations[layer_index])
        )
        mirror = jnp.transpose(exchanged(gradient, 1 + layer_index), (1, 0, 2))
        symmetric = ((gradient.astype(jnp.float32) + mirror.astype(jnp.float32)) * 0.5).astype(
            jnp.bfloat16
        )
        padded = padded_symmetric(symmetric, dilation, 1 + layers + layer_index)
        stacked = tap_columns(padded, height, extent, dilation)
        partial_value = (
            jnp.einsum("yxi,yxko->kio", inputs_now, stacked, preferred_element_type=jnp.float32)
            / map_side
        )
        input_change = jnp.einsum(
            "yxko,kio->yxi", stacked, weights[layer_index], preferred_element_type=jnp.float32
        )
        gradient = (
            gradient.astype(jnp.float32) + jnp.where(mask_now, input_change, jnp.float32(0.0))
        ).astype(jnp.bfloat16)
        collected.append(partial_value)
    kernel_stack = reduced(jnp.stack(collected[::-1]), 1 + 2 * layers)
    return (gradient, kernel_stack)


def solution(mesh):
    in_specs = (
        P("row", "col", None),
        P(None, "row", "col", None),
        P(None, "row", "col", None),
        P(),
    )
    out_specs = (P("row", "col", None), P())
    return jax.shard_map(
        per_device, mesh=mesh, in_specs=in_specs, out_specs=out_specs, check_vma=False
    )
```

time: 378 us -> 226 us (0.60)
  Pallas kernels: 0 us -> 183 us
  blocking collectives: 168 us -> 0 us
  waiting for transfers between devices: 149 us -> 0 us
  starting transfers between devices: 18.2 us -> 0 us
  between operations: 14.6 us -> 1 us
  other arithmetic: 4.35 us -> 12.4 us
  local copies, waits for them, and re-layouts: 8.85 us -> 16.5 us
    pallas_call x0 -> x7, Pallas kernels: none -> 183 us  [the longest x3 130 us: exchanged(): pl.pallas_call(functools.partial(exchange_kernel, chips, cols), out_shape...]
    all_to_all x9 -> x0, blocking collectives: 168 us -> none  [the longest x3 58.2 us: mirrored(): lax.all_to_all(local_tile, 'col', split_axis=0, concat_axis=1, tiled=True)]
    psum x1 -> x0, waiting for transfers between devices: 131 us -> none  [per_device(): collected.append(lax.psum(partial_value, ('row', 'col')))]
    ppermute x12 -> x0, waiting for transfers between devices: 18.7 us -> none  [the longest x6 18.5 us: extended(): lax.ppermute(lax.slice_in_dim(block, 0, width, axis=dim), axis, backward)]
    ppermute x12 -> x0, starting transfers between devices: 18.2 us -> none  [the longest x6 10.2 us: extended(): lax.ppermute(lax.slice_in_dim(block, block.shape[dim] - width, None, axis...]
    transpose x0 -> x9, local copies, waits for them, and re-layouts: none -> 4.72 us  [the longest x6 2.49 us: padded_symmetric(): pieces.append(jnp.transpose(piece, (1, 0, 2)) if y == 0 else piece)]
    dot_general x3, matrix products: 6.77 us -> 2.77 us  [per_device(): jnp.einsum('yxi,yxko->kio', inputs_now, stacked, preferred_element_type=j...]
  transfers between devices with their start and end apart: 13 -> 0, of which waited for: 8 -> 0; matrix products, arithmetic and copies ran while one was open for 3% -> 0% of each run, Pallas kernels for 0% -> 0%
where the time goes in v1:
time: 226 us; the launch traced here: 225 us
  Pallas kernels  183 us (81%)
  local copies, waits for them, and re-layouts  16.5 us (7%)
  other arithmetic  12.4 us (5%)
  matrix products  12.3 us (5%)
    pallas_call x3, Pallas kernels, exchanged(): pl.pallas_call(functools.partial(exchange_kernel, chips, cols), out_shape...  130 us
    pallas_call x1, Pallas kernels, reduced(): pl.pallas_call(functools.partial(reduce_kernel, layers, chips, cols), out...  26.9 us
    pallas_call x3, Pallas kernels, padded_symmetric(): pl.pallas_call(functools.partial(halo_kernel, lax.axis_size('row'), lax.a...  26.3 us
    dot_general x3, matrix products, per_device(): jnp.einsum('yxko,kio->yxi', stacked, weights[layer_index], preferred_elem...  9.57 us

profile of v1, /device:TPU:0, one launch (start us, length us, event | category | flops | bytes accessed | tf_op | source)
XLA Modules:
  0.0 225.1 jit_solution(14094770465000444181)
XLA Ops:
  0.6 44.0 %shard_map.59 = bf16[64,32,128]{2,1,0:T(8,128)(2,1)} custom-call(bf16[32,64,128]{2,1,0:T(8,128)(2,1)} %g.1), custom_call_target="tpu_custom_call" | custom-call | tf_op jit(solution)/shard_map/pallas_call | solution.py:117
  44.7 1.4 fusion.16
  48.7 8.9 %shard_map.60 = (bf16[4,4,128]{2,1,0:T(4,128)(2,1)}, bf16[4,64,128]{2,1,0:T(8,128)(2,1)}, bf16[4,4,128]{2,1,0:T(4,128)(2,1)}, bf16[4,32,128]{2,1,0:T(8,128)(2,1)...) custom-call(bf16[4,4,128]{2,1,0:T(4,128)(2,1)} %get-tuple-element.78, ...), custom_call_target="tpu_custom_call" | custom-call | tf_op jit(solution)/shard_map/pallas_call | solution.py:190
  57.5 0.8 copy_bitcast_fusion
  58.3 2.3 %fusion.21 = (pred[32,64,128]{2,1,0:T(32,128)(4,1)S(1)}, pred[32,64,128]{2,1,0:T(32,128)(4,1)S(1)}, pred[32,64,128]{2,1,0:T(32,128)(4,1)S(1)}) fusion(s32[3,32,64,128]{3,2,1,0:T(8,128)} %param.6), kind=kLoop, calls=%fused_computation.36 | loop fusion | flops 786432 | bytes 3932160 | tf_op jit(solution)/shard_map/gt | solution.py:352
  60.6 1.2 maximum_maximum_fusion.1
  63.3 0.9 fusion.12
  64.2 3.2 %fusion.3.g = bf16[32,64,128]{2,1,0:T(8,128)(2,1)} fusion(pred[32,64,128]{2,1,0:T(32,128)(4,1)S(1)} %get-tuple-element.50, bf16[32,64,9,128]{3,1,0,2:T(8,128)(2,1)S(1)} %fusion.44, bf16[32,64,128]{2,1,0:T(8,128)(2,1)S(1)} %copy-done, bf16[3,9,128,128]{3,2,1,0:T(8,128)(2,1)} %param.7), kind=kOutput, calls=%fused_computation.12 | convolution fusion | flops 605028352 | bytes 6324224 | tf_op jit(solution)/shard_map/yxko,kio->yxi/dot_general | solution.py:366
  67.5 42.8 %shard_map.61 = bf16[64,32,128]{2,1,0:T(8,128)(2,1)} custom-call(bf16[32,64,128]{2,1,0:T(8,128)(2,1)} %fusion.3.g), custom_call_target="tpu_custom_call" | custom-call | tf_op jit(solution)/shard_map/pallas_call | solution.py:117
  110.2 1.4 fusion.18
  114.2 8.7 %shard_map.62 = (bf16[2,2,128]{2,1,0:T(2,128)(2,1)}, bf16[2,64,128]{2,1,0:T(8,128)(2,1)}, bf16[2,2,128]{2,1,0:T(2,128)(2,1)}, bf16[2,32,128]{2,1,0:T(8,128)(2,1)...) custom-call(bf16[2,2,128]{2,1,0:T(2,128)(2,1)} %get-tuple-element.70, ...), custom_call_target="tpu_custom_call" | custom-call | tf_op jit(solution)/shard_map/pallas_call | solution.py:190
  122.8 0.7 copy.59
  124.3 1.1 maximum_maximum_fusion.3
  127.0 3.2 %fusion.4.g = bf16[32,64,128]{2,1,0:T(8,128)(2,1)} fusion(pred[32,64,128]{2,1,0:T(32,128)(4,1)S(1)} %get-tuple-element.52, bf16[32,64,9,128]{3,1,0,2:T(8,128)(2,1)S(1)} %fusion.34, bf16[32,64,128]{2,1,0:T(8,128)(2,1)S(1)} %copy-done.2, bf16[3,9,128,128]{3,2,1,0:T(8,128)(2,1)} %param.7), kind=kOutput, calls=%fused_computation.13 | convolution fusion | flops 605028352 | bytes 6324224 | tf_op jit(solution)/shard_map/yxko,kio->yxi/dot_general | solution.py:366
  130.2 0.9 fusion.13
  131.2 42.8 %shard_map.63 = bf16[64,32,128]{2,1,0:T(8,128)(2,1)} custom-call(bf16[32,64,128]{2,1,0:T(8,128)(2,1)} %fusion.4.g), custom_call_target="tpu_custom_call" | custom-call | tf_op jit(solution)/shard_map/pallas_call | solution.py:117
  174.0 1.3 fusion.20
  177.8 8.8 %shard_map.64 = (bf16[1,1,128]{2,1,0:T(2,128)(2,1)}, bf16[1,64,128]{2,1,0:T(8,128)(2,1)}, bf16[1,1,128]{2,1,0:T(2,128)(2,1)}, bf16[1,32,128]{2,1,0:T(8,128)(2,1)...) custom-call(bf16[1,1,128]{2,1,0:T(2,128)(2,1)} %get-tuple-element.62, ...), custom_call_target="tpu_custom_call" | custom-call | tf_op jit(solution)/shard_map/pallas_call | solution.py:190
  188.0 1.1 maximum_maximum_fusion.5
  190.6 3.2 %fusion.5 = bf16[32,64,128]{2,1,0:T(8,128)(2,1)} fusion(pred[32,64,128]{2,1,0:T(32,128)(4,1)S(1)} %get-tuple-element.51, bf16[32,64,9,128]{3,1,0,2:T(8,128)(2,1)S(1)} %fusion.24, bf16[32,64,128]{2,1,0:T(8,128)(2,1)S(1)} %copy-done.1, bf16[3,9,128,128]{3,2,1,0:T(8,128)(2,1)} %param.7), kind=kOutput, calls=%fused_computation.14 | convolution fusion | flops 605028352 | bytes 6324224 | tf_op jit(solution)/shard_map/yxko,kio->yxi/dot_general | solution.py:366
  193.8 0.9 fusion.14
  194.8 1.1 pad_maximum_fusion.x
  195.8 26.9 %shard_map.65 = bf16[3,2,4,4,36,128]{5,4,3,2,1,0:T(8,128)(2,1)} custom-call(bf16[3,2,4,4,36,128]{5,4,3,2,1,0:T(8,128)(2,1)} %pad_maximum_fusion.x), custom_call_target="tpu_custom_call" | custom-call | tf_op jit(solution)/shard_map/pallas_call | solution.py:307
  222.8 2.4 %reshape.23 = f32[3,9,128,128]{3,2,1,0:T(8,128)} reshape(bf16[3,2,4,4,36,128]{5,4,3,2,1,0:T(8,128)(2,1)} %shard_map.65) | data formatting | bytes 2654208 | tf_op jit(solution)/shard_map/convert_element_type | solution.py:329
  (56 shorter events, 14.1 us)
Async XLA Ops:
  61.8 1.4 copy-start.3
  63.1 1.1 copy-start
  125.4 1.6 copy-start.2
  130.2 43.8 %copy-start.1 = (bf16[32,64,128]{2,1,0:T(8,128)(2,1)S(1)}, bf16[32,64,128]{2,1,0:T(8,128)(2,1)}, u32[]{:S(2)}) copy-start(bf16[32,64,128]{2,1,0:T(8,128)(2,1)} %fusion.4.g) | copy-start | bytes 1572868

commit v2 on v1

--- a/solution.py
+++ b/solution.py
@@ -9,8 +9,6 @@
 
 MESH = pl.DeviceIdType.MESH
 VMEM = pl.BlockSpec(memory_space=pltpu.VMEM)
-LATE = True
-
 
 def remote(src, dst, send, recv, row, col):
     return pltpu.make_async_remote_copy(
@@ -23,26 +21,16 @@
     )
 
 
-def exchange_kernel(chips, cols, g, arrived, relay, send_a, recv_a, send_b, recv_b):
+def exchange_kernel(count, chips, cols, *refs):
+    fields, arrived = refs[:count], refs[count : 2 * count]
+    relay, send_a, recv_a, send_b, recv_b = refs[2 * count :]
     row, col = lax.axis_index("row"), lax.axis_index("col")
     chip, core = lax.div(row, 2), lax.rem(row, 2)
-    height, extent, _ = g.shape
+    height, extent, _ = fields[0].shape
     half = extent // 2
     part = height // chips
     barrier = pltpu.get_barrier_semaphore()
 
-    def first_target(b):
-        return (2 * b + core, chip) if LATE else (2 * b + core, col)
-
-    def first_source(k):
-        return (2 * col + core, k) if LATE else (2 * k + core, col)
-
-    def second_target(k, h):
-        return (2 * k + h, col) if LATE else (2 * col + h, k)
-
-    def second_source(b, h):
-        return (2 * b + h, col) if LATE else (2 * b + h, chip)
-
     def other(place):
         return jnp.logical_or(place[0] != row, place[1] != col)
 
@@ -51,29 +39,33 @@
         def _():
             pl.semaphore_signal(barrier, inc=1, device_id=place, device_id_type=MESH)
 
+    def first_place(j):
+        return 2 * lax.rem(chip + j, chips) + core, col
+
+    def second_place(j, h):
+        return 2 * col + h, lax.rem(col + j, cols)
+
     for k in range(chips):
-        signal(first_source(k))
+        signal((2 * k + core, col))
         for h in range(2):
-            signal(second_source(k, h))
+            signal((2 * k + h, chip))
     expected = jnp.int32(0)
-    for k in range(chips):
-        expected += other(first_target(k)).astype(jnp.int32)
+    for j in range(chips):
+        expected += other(first_place(j)).astype(jnp.int32)
         for h in range(2):
-            expected += other(second_target(k, h)).astype(jnp.int32)
+            expected += other(second_place(j, h)).astype(jnp.int32)
     pl.semaphore_wait(barrier, expected)
 
-    slot = col if LATE else chip
-
-    def first(b):
-        place = first_target(b)
-        src = g.at[pl.ds(b * part, part)]
-        return place, src, relay.at[slot], send_a.at[b], recv_a.at[slot]
-
-    def second(k, h):
-        place = second_target(k, h)
-        src = relay.at[k, :, pl.ds(h * half, half)]
-        dst = arrived.at[pl.ds(core * height + chip * part, part)]
-        return place, src, dst, send_b.at[2 * k + h], recv_b.at[row]
+    def first(t, j):
+        place = first_place(j)
+        src = fields[t].at[pl.ds(lax.rem(chip + j, chips) * part, part)]
+        return place, src, relay.at[t, chip], send_a.at[t, j], recv_a.at[t, chip]
+
+    def second(t, j, h):
+        place = second_place(j, h)
+        src = relay.at[t, place[1], :, pl.ds(h * half, half)]
+        dst = arrived[t].at[pl.ds(core * height + chip * part, part)]
+        return place, src, dst, send_b.at[t, 2 * j + h], recv_b.at[t, row]
 
     def begin(item):
         place, src, dst, send, recv = item
@@ -94,42 +86,51 @@
         def _():
             remote(src, dst, send, recv, *place).wait_send()
 
-    for b in range(chips):
-        begin(first(b))
-    for k in range(chips):
-        pltpu.make_async_copy(relay.at[k], relay.at[k], recv_a.at[k]).wait()
-        for h in range(2):
-            begin(second(k, h))
-    for b in range(chips):
-        finish(first(b))
-        for h in range(2):
-            finish(second(b, h))
-    for b in range(chips):
-        for h in range(2):
-            dst = arrived.at[pl.ds(h * height + b * part, part)]
-            pltpu.make_async_copy(dst, dst, recv_b.at[2 * b + h]).wait()
-
-
-def exchanged(gradient, index):
-    height, extent, channels = gradient.shape
+    for t in range(count):
+        for j in range(chips):
+            begin(first(t, j))
+    for t in range(count):
+        for j in range(cols):
+            k = lax.rem(col + j, cols)
+            slab = relay.at[t, k]
+            pltpu.make_async_copy(slab, slab, recv_a.at[t, k]).wait()
+            for h in range(2):
+                begin(second(t, j, h))
+    for t in range(count):
+        for j in range(chips):
+            finish(first(t, j))
+            for h in range(2):
+                finish(second(t, j, h))
+    for t in range(count):
+        for b in range(chips):
+            for h in range(2):
+                dst = arrived[t].at[pl.ds(h * height + b * part, part)]
+                pltpu.make_async_copy(dst, dst, recv_b.at[t, 2 * b + h]).wait()
+
+
+def mirrored(fields, index):
+    height, extent, channels = fields[0].shape
+    kind = fields[0].dtype
     rows, cols = lax.axis_size("row"), lax.axis_size("col")
-    chips = rows // 2
-    return pl.pallas_call(
-        functools.partial(exchange_kernel, chips, cols),
-        out_shape=jax.ShapeDtypeStruct((extent, height, channels), gradient.dtype),
-        in_specs=[VMEM],
-        out_specs=VMEM,
+    chips, count = rows // 2, len(fields)
+    dma = pltpu.SemaphoreType.DMA
+    got = pl.pallas_call(
+        functools.partial(exchange_kernel, count, chips, cols),
+        out_shape=[jax.ShapeDtypeStruct((extent, height, channels), kind)] * count,
+        in_specs=[VMEM] * count,
+        out_specs=[VMEM] * count,
         scratch_shapes=[
-            pltpu.VMEM((chips, height // chips, extent, channels), gradient.dtype),
-            pltpu.SemaphoreType.DMA((chips,)),
-            pltpu.SemaphoreType.DMA((chips,)),
-            pltpu.SemaphoreType.DMA((rows,)),
-            pltpu.SemaphoreType.DMA((rows,)),
+            pltpu.VMEM((count, chips, height // chips, extent, channels), kind),
+            dma((count, chips)),
+            dma((count, chips)),
+            dma((count, rows)),
+            dma((count, rows)),
         ],
         compiler_params=pltpu.CompilerParams(
             collective_id=index, has_side_effects=True
         ),
-    )(gradient)
+    )(*fields)
+    return [jnp.transpose(field, (1, 0, 2)) for field in got]
 
 
 SIDES = [(-1, -1), (-1, 0), (-1, 1), (0, -1), (0, 1), (1, -1), (1, 0), (1, 1)]
@@ -345,32 +346,40 @@
     height, extent, channels = cotangent.shape
     map_side = height * lax.axis_size("row")
     layers = weights.shape[0]
-    gradient = cotangent
+    wide = jnp.float32
+    masks = [active_masks[n] > 0 for n in range(layers)]
+    fields = [cotangent] + [masks[n].astype(cotangent.dtype) for n in range(layers - 1, 0, -1)]
+    mirrors = mirrored(fields, 1)
+    gradient, opposite = cotangent, mirrors[0]
     collected = []
     for layer_index in reversed(range(layers)):
         dilation = 2**layer_index
-        mask_now = active_masks[layer_index] > 0
+        mask_now = masks[layer_index]
         inputs_now = jnp.where(
             mask_now, activations[layer_index], jnp.zeros_like(activations[layer_index])
         )
-        mirror = jnp.transpose(exchanged(gradient, 1 + layer_index), (1, 0, 2))
-        symmetric = ((gradient.astype(jnp.float32) + mirror.astype(jnp.float32)) * 0.5).astype(
-            jnp.bfloat16
-        )
-        padded = padded_symmetric(symmetric, dilation, 1 + layers + layer_index)
+        symmetric = ((gradient.astype(wide) + opposite.astype(wide)) * 0.5).astype(jnp.bfloat16)
+        padded = padded_symmetric(symmetric, dilation, 2 + layer_index)
         stacked = tap_columns(padded, height, extent, dilation)
+        kernels = weights[layer_index]
+        if layer_index:
+            swapped = kernels.reshape(3, 3, channels, channels).swapaxes(0, 1)
+            kernels = jnp.concatenate([kernels, swapped.reshape(9, channels, channels)], axis=1)
+        change = jnp.einsum("yxko,kio->yxi", stacked, kernels, preferred_element_type=wide)
         partial_value = (
-            jnp.einsum("yxi,yxko->kio", inputs_now, stacked, preferred_element_type=jnp.float32)
+            jnp.einsum("yxi,yxko->kio", inputs_now, stacked, preferred_element_type=wide)
             / map_side
         )
-        input_change = jnp.einsum(
-            "yxko,kio->yxi", stacked, weights[layer_index], preferred_element_type=jnp.float32
-        )
         gradient = (
-            gradient.astype(jnp.float32) + jnp.where(mask_now, input_change, jnp.float32(0.0))
+            gradient.astype(wide) + jnp.where(mask_now, change[..., :channels], wide(0.0))
         ).astype(jnp.bfloat16)
+        if layer_index:
+            mask_there = mirrors[layers - layer_index] > 0
+            opposite = (
+                opposite.astype(wide) + jnp.where(mask_there, change[..., channels:], wide(0.0))
+            ).astype(jnp.bfloat16)
         collected.append(partial_value)
-    kernel_stack = reduced(jnp.stack(collected[::-1]), 1 + 2 * layers)
+    kernel_stack = reduced(jnp.stack(collected[::-1]), 2 + layers)
     return (gradient, kernel_stack)
 
 

time: 226 us -> 147 us (0.65)
  Pallas kernels: 183 us -> 101 us
  local copies, waits for them, and re-layouts: 16.5 us -> 18.9 us
    pallas_call x3 -> x1, Pallas kernels: 130 us -> 51.5 us  [mirrored(): pl.pallas_call(functools.partial(exchange_kernel, count, chips, cols), ou...]
    pallas_call x3, Pallas kernels: 26.3 us -> 21.3 us  [padded_symmetric(): pl.pallas_call(functools.partial(halo_kernel, lax.axis_size('row'), lax.a...]
    gt x1 -> x0, other arithmetic: 2.3 us -> none  [per_device(): mask_now = active_masks[layer_index] > 0]
    convert_element_type x3 -> x4, other arithmetic: 4.19 us -> 6.02 us  [the longest x1 3.46 us: per_device(): masks[n].astype(cotangent.dtype)]
where the time goes in v2:
time: 147 us; the launch traced here: 146 us
  Pallas kernels  101 us (69%)
  local copies, waits for them, and re-layouts  18.9 us (13%)
  matrix products  13.7 us (9%)
  other arithmetic  12 us (8%)
    pallas_call x1, Pallas kernels, mirrored(): pl.pallas_call(functools.partial(exchange_kernel, count, chips, cols), ou...  51.5 us
    pallas_call x1, Pallas kernels, reduced(): pl.pallas_call(functools.partial(reduce_kernel, layers, chips, cols), out...  27.8 us
    pallas_call x3, Pallas kernels, padded_symmetric(): pl.pallas_call(functools.partial(halo_kernel, lax.axis_size('row'), lax.a...  21.3 us
    dot_general x3, matrix products, per_device(): jnp.einsum('yxi,yxko->kio', inputs_now, stacked, preferred_element_type=w...  7.35 us
    dot_general x3, matrix products, per_device(): jnp.einsum('yxko,kio->yxi', stacked, kernels, preferred_element_type=wide)  6.38 us
    unnamed x32, local copies, waits for them, and re-layouts  3.79 us
    slice x7, local copies, waits for them, and re-layouts, padded_symmetric(): piece = symmetric[down[y], down[x]]  3.73 us
    convert_element_type x1, other arithmetic, per_device(): masks[n].astype(cotangent.dtype)  3.46 us

profile of v2, /device:TPU:0, one launch (start us, length us, event | category | flops | bytes accessed | tf_op | source)
XLA Modules:
  0.0 146.3 jit_solution(12339770235902652349)
XLA Ops:
  0.6 1.4 slice_bitcast_fusion.22
  2.1 3.5 %fusion.78 = (bf16[32,64,128]{2,1,0:T(8,128)(2,1)}, pred[32,64,128]{2,1,0:T(32,128)(4,1)S(1)}, bf16[32,64,128]{2,1,0:T(8,128)(2,1)}, pred[32,64,128]{2,1,0:T(32,128)(4,1)S(1)}, pred[32,64,128]{2,1,0:T(32,128)(4,1)}) fusion(s32[3,32,64,128]{3,2,1,0:T(8,128)} %param.6), kind=kLoop, calls=%fused_computation.146 | loop fusion | flops 1310720 | bytes 4980736 | tf_op jit(solution)/shard_map/convert_element_type | solution.py:351
  5.6 51.5 %shard_map.59 = (bf16[64,32,128]{2,1,0:T(8,128)(2,1)}, bf16[64,32,128]{2,1,0:T(8,128)(2,1)}, bf16[64,32,128]{2,1,0:T(8,128)(2,1)}) custom-call(bf16[32,64,128]{2,1,0:T(8,128)(2,1)} %refs_0_.1, bf16[32,64,128]{2,1,0:T(8,128)(2,1)} %get-tuple-element.65.refs_1_, bf16[32,64,128]{2,1,0:T(8,128)(2,1)} %get-tuple-element.61.refs_2_), custom_call_target="tpu_custom_call" | custom-call | tf_op jit(solution)/shard_map/pallas_call | solution.py:117
  57.0 1.3 fusion.12
  60.9 8.4 %shard_map.60 = (bf16[4,4,128]{2,1,0:T(4,128)(2,1)}, bf16[4,64,128]{2,1,0:T(8,128)(2,1)}, bf16[4,4,128]{2,1,0:T(4,128)(2,1)}, bf16[4,32,128]{2,1,0:T(8,128)(2,1)...) custom-call(bf16[4,4,128]{2,1,0:T(4,128)(2,1)} %get-tuple-element.97, ...), custom_call_target="tpu_custom_call" | custom-call | tf_op jit(solution)/shard_map/pallas_call | solution.py:191
  69.3 0.8 copy_bitcast_fusion
  70.1 1.2 maximum_maximum_fusion.1
  72.7 2.7 %fusion.8 = bf16[9,128,128]{2,1,0:T(8,128)(2,1)} fusion(bf16[32,64,9,128]{3,1,0,2:T(8,128)(2,1)S(1)} %fusion.49, pred[32,64,128]{2,1,0:T(32,128)(4,1)S(1)} %get-tuple-element.66, bf16[3,32,64,128]{3,2,1,0:T(8,128)(2,1)} %param.5), kind=kOutput, calls=%fused_computation.21 | convolution fusion | flops 604536832 | bytes 5799936 | tf_op jit(solution)/shard_map/yxi,yxko->kio/dot_general | solution.py:370
  75.4 1.6 %convolution_bitcast_fusion.1 = f32[32,64,256]{2,1,0:T(8,128)S(1)} fusion(bf16[32,64,9,128]{3,1,0,2:T(8,128)(2,1)S(1)} %fusion.49, bf16[9,128,128]{2,1,0:T(8,128)(2,1)S(1)} %bitcast.253, bf16[9,128,128]{2,1,0:T(8,128)(2,1)S(1)} %get-tuple-element.69), kind=kOutput, calls=%fused_computation.1 | convolution fusion | flops 1209139200 | bytes 7405568 | tf_op jit(solution)/shard_map/yxko,kio->yxi/dot_general | solution.py:368
  78.3 1.0 stack.134
  81.2 7.5 %shard_map.61 = (bf16[2,2,128]{2,1,0:T(2,128)(2,1)}, bf16[2,64,128]{2,1,0:T(8,128)(2,1)}, bf16[2,2,128]{2,1,0:T(2,128)(2,1)}, bf16[2,32,128]{2,1,0:T(8,128)(2,1)...) custom-call(bf16[2,2,128]{2,1,0:T(2,128)(2,1)} %get-tuple-element.89, ...), custom_call_target="tpu_custom_call" | custom-call | tf_op jit(solution)/shard_map/pallas_call | solution.py:191
  88.7 0.7 copy.66
  89.5 0.7 copy.65
  90.2 1.1 maximum_maximum_fusion.3
  92.9 2.7 %fusion.9 = bf16[9,128,128]{2,1,0:T(8,128)(2,1)} fusion(bf16[32,64,9,128]{3,1,0,2:T(8,128)(2,1)S(1)} %fusion.39, pred[32,64,128]{2,1,0:T(32,128)(4,1)S(1)} %get-tuple-element.62, bf16[3,32,64,128]{3,2,1,0:T(8,128)(2,1)} %param.5), kind=kOutput, calls=%fused_computation.22 | convolution fusion | flops 604536832 | bytes 5799936 | tf_op jit(solution)/shard_map/yxi,yxko->kio/dot_general | solution.py:370
  95.6 1.6 %convolution_bitcast_fusion = f32[32,64,256]{2,1,0:T(8,128)S(1)} fusion(bf16[32,64,9,128]{3,1,0,2:T(8,128)(2,1)S(1)} %fusion.39, bf16[9,128,128]{2,1,0:T(8,128)(2,1)S(1)} %bitcast.252, bf16[9,128,128]{2,1,0:T(8,128)(2,1)S(1)} %get-tuple-element.68), kind=kOutput, calls=%fused_computation | convolution fusion | flops 1209139200 | bytes 7405568 | tf_op jit(solution)/shard_map/yxko,kio->yxi/dot_general | solution.py:368
  100.3 5.4 %shard_map.62 = (bf16[1,1,128]{2,1,0:T(2,128)(2,1)}, bf16[1,64,128]{2,1,0:T(8,128)(2,1)}, bf16[1,1,128]{2,1,0:T(2,128)(2,1)}, bf16[1,32,128]{2,1,0:T(8,128)(2,1)...) custom-call(bf16[1,1,128]{2,1,0:T(2,128)(2,1)} %get-tuple-element.81, ...), custom_call_target="tpu_custom_call" | custom-call | tf_op jit(solution)/shard_map/pallas_call | solution.py:191
  105.8 0.7 copy.38
  107.2 1.1 maximum_maximum_fusion.5
  109.8 3.2 %fusion.1 = bf16[32,64,128]{2,1,0:T(8,128)(2,1)} fusion(pred[32,64,128]{2,1,0:T(32,128)(4,1)S(1)} %copy-done.5, bf16[32,64,9,128]{3,1,0,2:T(8,128)(2,1)S(1)} %fusion.29, bf16[32,64,128]{2,1,0:T(8,128)(2,1)S(1)} %get-tuple-element.57, bf16[3,9,128,128]{3,2,1,0:T(8,128)(2,1)} %param.7), kind=kOutput, calls=%fused_computation.11 | convolution fusion | flops 605028352 | bytes 6324224 | tf_op jit(solution)/shard_map/yxko,kio->yxi/dot_general | solution.py:368
  113.0 2.0 %fusion.10 = bf16[9,128,128]{2,1,0:T(8,128)(2,1)S(1)} fusion(bf16[32,64,9,128]{3,1,0,2:T(8,128)(2,1)S(1)} %fusion.29, pred[32,64,128]{2,1,0:T(32,128)(4,1)S(1)} %copy-done.5, bf16[3,32,64,128]{3,2,1,0:T(8,128)(2,1)} %param.5), kind=kOutput, calls=%fused_computation.23 | convolution fusion | flops 604536832 | bytes 5799936 | tf_op jit(solution)/shard_map/yxi,yxko->kio/dot_general | solution.py:370
  115.1 1.1 pad_maximum_fusion.x
  116.1 27.8 %shard_map.63 = bf16[3,2,4,4,36,128]{5,4,3,2,1,0:T(8,128)(2,1)} custom-call(bf16[3,2,4,4,36,128]{5,4,3,2,1,0:T(8,128)(2,1)} %pad_maximum_fusion.x), custom_call_target="tpu_custom_call" | custom-call | tf_op jit(solution)/shard_map/pallas_call | solution.py:308
  143.9 2.4 %reshape.31 = f32[3,9,128,128]{3,2,1,0:T(8,128)} reshape(bf16[3,2,4,4,36,128]{5,4,3,2,1,0:T(8,128)(2,1)} %shard_map.63) | data formatting | bytes 2654208 | tf_op jit(solution)/shard_map/convert_element_type | solution.py:330
  (61 shorter events, 13.9 us)
Async XLA Ops:
  0.6 56.4 %copy-start = (bf16[32,64,128]{2,1,0:T(8,128)(2,1)S(1)}, bf16[32,64,128]{2,1,0:T(8,128)(2,1)}, u32[]{:S(2)}) copy-start(bf16[32,64,128]{2,1,0:T(8,128)(2,1)} %refs_0_.1) | copy-start | bytes 1572868
  75.4 1.6 %copy-start.1 = (bf16[64,32,128]{2,1,0:T(8,128)(2,1)S(1)}, bf16[64,32,128]{2,1,0:T(8,128)(2,1)}, u32[]{:S(2)}) copy-start(bf16[64,32,128]{2,1,0:T(8,128)(2,1)} %get-tuple-element.29) | copy-start | bytes 1572868
  75.4 1.6 %copy-start.3 = (bf16[64,32,128]{2,1,0:T(8,128)(2,1)S(1)}, bf16[64,32,128]{2,1,0:T(8,128)(2,1)}, u32[]{:S(2)}) copy-start(bf16[64,32,128]{2,1,0:T(8,128)(2,1)} %get-tuple-element.38) | copy-start | bytes 1572868
  95.6 1.6 %copy-start.2 = (bf16[64,32,128]{2,1,0:T(8,128)(2,1)S(1)}, bf16[64,32,128]{2,1,0:T(8,128)(2,1)}, u32[]{:S(2)}) copy-start(bf16[64,32,128]{2,1,0:T(8,128)(2,1)} %get-tuple-element.47) | copy-start | bytes 1572868
  97.2 1.2 copy-start.4
  108.3 1.5 %copy-start.5 = (pred[32,64,128]{2,1,0:T(32,128)(4,1)S(1)}, pred[32,64,128]{2,1,0:T(32,128)(4,1)}, u32[]{:S(2)}) copy-start(pred[32,64,128]{2,1,0:T(32,128)(4,1)} %get-tuple-element.67) | copy-start | bytes 786436

commit v3 on v0

v3 whole, which is shorter than its diff:
```python
import functools

import jax
import jax.numpy as jnp
from jax import lax
from jax.experimental import pallas as pl
from jax.experimental.pallas import tpu as pltpu
from jax.sharding import PartitionSpec as P

MESH = pl.DeviceIdType.MESH
VMEM = pl.BlockSpec(memory_space=pltpu.VMEM)
WIDE = jnp.float32
NARROW = jnp.bfloat16
EDGE = 16
CHUNK = 8
SIDES = [(-1, -1), (-1, 0), (-1, 1), (0, -1), (0, 1), (1, -1), (1, 0), (1, 1)]


def remote(src, dst, send, recv, row, col):
    return pltpu.make_async_remote_copy(
        src_ref=src,
        dst_ref=dst,
        send_sem=send,
        recv_sem=recv,
        device_id=(row, col),
        device_id_type=MESH,
    )


def whole_kernel(layers, rows, cols, share, slab, *refs):
    cotangent, activations, masks, kernels, gradient, total = refs[:6]
    (
        fields, relay, arrived, opposite, there, padded, shifted, x, r1, s1, r2, s2, r3, z,
        send_a, recv_a, send_b, recv_b, send_h, recv_h, send1, recv1, send2, recv2,
        send3, recv3, send4, recv4, send5, recv5, send6, recv6,
    ) = refs[6:]
    chips = rows // 2
    row, col = lax.axis_index("row"), lax.axis_index("col")
    chip, core = lax.div(row, 2), lax.rem(row, 2)
    sibling = 2 * chip + 1 - core
    height, extent, channels = cotangent.shape
    half, part = extent // 2, height // chips
    rim = (padded.shape[1] - height) // 2
    side = height * rows
    breadth = extent + 2 * EDGE

    @pl.loop(0, height // CHUNK)
    def _(n):
        at = pl.ds(n * CHUNK, CHUNK)
        for t in range(layers - 1):
            fields[t, at] = masks[layers - 1 - t, at].astype(WIDE).astype(NARROW)

    padded[...] = jnp.zeros_like(padded)
    s2[...] = jnp.zeros_like(s2)
    x[...] = jnp.zeros_like(x)

    barrier = pltpu.get_barrier_semaphore()

    @pl.loop(0, rows)
    def _(r):
        for c in range(cols):

            @pl.when(jnp.logical_or(r != row, c != col))
            def _():
                pl.semaphore_signal(barrier, inc=1, device_id=(r, c), device_id_type=MESH)

    pl.semaphore_wait(barrier, rows * cols - 1)

    def other(place):
        return jnp.logical_or(place[0] != row, place[1] != col)

    def first(t, j):
        b = lax.rem(chip + j, chips)
        field = cotangent if t == 0 else fields.at[t - 1]
        src = field.at[pl.ds(b * part, part)]
        return (2 * b + core, col), src, relay.at[t, chip], send_a.at[t, j], recv_a.at[t, chip]

    def second(t, j, h):
        k = lax.rem(col + j, cols)
        src = relay.at[t, k, :, pl.ds(h * half, half)]
        dst = arrived.at[t, pl.ds(core * height + chip * part, part)]
        return (2 * col + h, k), src, dst, send_b.at[t, 2 * j + h], recv_b.at[t, row]

    def begin(item):
        place, src, dst, send, recv = item
        away = other(place)

        @pl.when(away)
        def _():
            remote(src, dst, send, recv, *place).start()

        @pl.when(jnp.logical_not(away))
        def _():
            pltpu.make_async_copy(src, dst, recv).start()

    def finish(item):
        place, src, dst, send, recv = item

        @pl.when(other(place))
        def _():
            remote(src, dst, send, recv, *place).wait_send()

    def forward(t):
        for j in range(cols):
            k = lax.rem(col + j, cols)
            pltpu.make_async_copy(relay.at[t, k], relay.at[t, k], recv_a.at[t, k]).wait()
            for h in range(2):
                begin(second(t, j, h))

    def collect(t, result):
        for b in range(chips):
            for h in range(2):
                dst = arrived.at[t, pl.ds(h * height + b * part, part)]
                pltpu.make_async_copy(dst, dst, recv_b.at[t, 2 * b + h]).wait()

        @pl.loop(0, extent // 16)
        def _(n):
            at = pl.ds(pl.multiple_of(n * 16, 16), 16)
            result[:, at] = jnp.swapaxes(arrived[t, at].astype(WIDE), 0, 1).astype(NARROW)

    def place_of(step):
        down, across = row + step[0], col + step[1]
        inside = jnp.logical_and(
            jnp.logical_and(down >= 0, down < rows),
            jnp.logical_and(across >= 0, across < cols),
        )
        return inside, down, across

    def spans(step, d, landing):
        y, w = step
        if landing:
            ys = {-1: (rim - d, d), 0: (rim, height), 1: (rim + height, d)}[y]
            xs = {-1: (0, EDGE), 0: (EDGE, extent), 1: (EDGE + extent, EDGE)}[w]
        else:
            ys = {-1: (rim, d), 0: (rim, height), 1: (rim + height - d, d)}[y]
            xs = {-1: (EDGE, EDGE), 0: (EDGE, extent), 1: (extent, EDGE)}[w]
        return pl.ds(*ys), pl.ds(*xs)

    def halo(l, n, receiver):
        step, d = SIDES[n], 2**l
        inside, down, across = place_of(step)
        src = padded.at[(l,) + spans(step, d, False)]
        if receiver:
            dst = padded.at[(l,) + spans(step, d, True)]
            return inside, remote(src, dst, send_h.at[l, n], recv_h.at[l, n], down, across)
        back = (-step[0], -step[1])
        dst = padded.at[(l,) + spans(back, d, True)]
        return inside, remote(src, dst, send_h.at[l, n], recv_h.at[l, 7 - n], down, across)

    def halo_start(l):
        for n in range(8):
            inside, copy = halo(l, n, False)
            pl.when(inside)(copy.start)

    def halo_wait(l):
        for n in range(8):
            inside, copy = halo(l, n, True)
            pl.when(inside)(copy.wait)

    def symmetrize(l, mine):
        @pl.loop(0, height // CHUNK)
        def _(n):
            at = pl.ds(n * CHUNK, CHUNK)
            both = mine[at].astype(WIDE) + opposite[at].astype(WIDE)
            padded[l, pl.ds(rim + n * CHUNK, CHUNK), pl.ds(EDGE, extent)] = (both * 0.5).astype(
                NARROW
            )

    def shift(l):
        d = 2**l

        @pl.loop(rim - d, rim + height + d)
        def _(r):
            line = padded[l, r].astype(WIDE)
            for b in range(3):
                moved = line
                if b != 1:
                    moved = pltpu.roll(line, (d * (b - 1)) % breadth, 0)
                shifted[l % 2, r, :, b * channels : (b + 1) * channels] = moved[
                    EDGE : EDGE + extent
                ].astype(NARROW)

    def cells(l, a, n):
        start = rim + 2**l * (1 - a) + n * CHUNK
        return shifted[l % 2, pl.ds(start, CHUNK)].reshape(CHUNK * extent, 3 * channels)

    def data(l, mine):
        @pl.loop(0, height // CHUNK)
        def _(n):
            at = pl.ds(n * CHUNK, CHUNK)
            change = jnp.zeros((CHUNK * extent, (2 if l else 1) * channels), WIDE)
            for a in range(3):
                weight = kernels[l, a] if l else kernels[l, a, :, :channels]
                change += jnp.dot(cells(l, a, n), weight, preferred_element_type=WIDE)
            own = change[:, :channels].reshape(CHUNK, extent, channels)
            new = mine[at].astype(WIDE) + jnp.where(masks[l, at] > 0, own, 0.0)
            gradient[at] = new.astype(NARROW)
            if l:
                own = change[:, channels:].reshape(CHUNK, extent, channels)
                open_ = there[at].astype(WIDE) > 0
                new = opposite[at].astype(WIDE) + jnp.where(open_, own, 0.0)
                opposite[at] = new.astype(NARROW)

    def weight(l):
        for a in range(3):

            @pl.loop(0, height // CHUNK)
            def _(n):
                at = pl.ds(n * CHUNK, CHUNK)
                inputs = jnp.where(masks[l, at] > 0, activations[l, at].astype(WIDE), 0.0)
                inputs = inputs.astype(NARROW).reshape(CHUNK * extent, channels)
                term = lax.dot_general(
                    inputs, cells(l, a, n), (((0,), (0,)), ((), ())), preferred_element_type=WIDE
                ) / side
                for b in range(3):
                    here = pl.ds((3 * a + b) * channels, channels)
                    x[l, here] += term[:, b * channels : (b + 1) * channels]

    def chip_at(j):
        return lax.rem(chip + j, chips)

    def col_at(j):
        return lax.rem(col + j, cols)

    def piece(core_at, k):
        return pl.ds(pl.multiple_of((core_at * chips + k) * share, 16), share)

    def wide_piece(core_at):
        return pl.ds(pl.multiple_of(core_at * chips * share, 16), chips * share)

    def slabs(k):
        return pl.ds(pl.multiple_of(k * slab, 16), slab)

    def p1(l):
        return remote(x.at[l, wide_piece(1 - core)], r1.at[l], send1.at[l], recv1.at[l], sibling, col)

    def p2(l, j):
        k = chip_at(j)
        src = s1.at[l, pl.ds(pl.multiple_of(k * share, 16), share)]
        return remote(src, r2.at[l, j], send2.at[l, j], recv2.at[l, j], 2 * k + core, col)

    def p3(l, j):
        k = col_at(j)
        return remote(s2.at[l, slabs(k)], r3.at[l, j], send3.at[l, j], recv3.at[l, j], row, k)

    def p4(l, j):
        mine = z.at[l, slabs(col)]
        return remote(mine, mine, send4.at[l, j], recv4.at[l, j], row, col_at(j))

    def p5(l, j):
        src, dst = z.at[l, pl.ds(0, share)], total.at[l, piece(core, chip)]
        return remote(src, dst, send5.at[l, j], recv5.at[l, j], 2 * chip_at(j) + core, col)

    def p6(l):
        mine = total.at[l, wide_piece(core)]
        return remote(mine, mine, send6.at[l], recv6.at[l], sibling, col)

    def sum1(l):
        p1(l).start()

    def sum2(l):
        p1(l).wait_recv()
        s1[l] = (x[l, wide_piece(core)] + r1[l]).astype(NARROW)
        for j in range(1, chips):
            p2(l, j).start()

    def sum3(l):
        value = s1[l, pl.ds(pl.multiple_of(chip * share, 16), share)].astype(WIDE)
        for j in range(1, chips):
            p2(l, j).wait_recv()
            value += r2[l, j].astype(WIDE)
        s2[l, pl.ds(0, share)] = value.astype(NARROW)
        for j in range(1, cols):
            p3(l, j).start()

    def sum4(l):
        value = s2[l, slabs(col)].astype(WIDE)
        for j in range(1, cols):
            p3(l, j).wait_recv()
            value += r3[l, j].astype(WIDE)
        z[l, slabs(col)] = value.astype(NARROW)
        for j in range(1, cols):
            p4(l, j).start()

    def sum5(l):
        for j in range(1, cols):
            p4(l, j).wait_recv()
        for j in range(1, chips):
            p5(l, j).start()
        total[l, piece(core, chip)] = z[l, pl.ds(0, share)]

    def sum6(l):
        for j in range(1, chips):
            p5(l, j).wait_recv()
        p6(l).start()

    def sum7(l):
        p6(l).wait_recv()
        p1(l).wait_send()
        p6(l).wait_send()
        for j in range(1, chips):
            p2(l, j).wait_send()
            p5(l, j).wait_send()
        for j in range(1, cols):
            p3(l, j).wait_send()
            p4(l, j).wait_send()

    for t in range(layers):
        for j in range(chips):
            begin(first(t, j))
    forward(0)
    for t in range(1, layers):
        forward(t)
    collect(0, opposite)
    pending = []

    def advance():
        for steps in pending:
            if steps:
                steps.pop(0)()

    top = layers - 1
    for l in range(top, -1, -1):
        mine = cotangent if l == top else gradient
        symmetrize(l, mine)
        halo_start(l)
        if l < top:
            weight(l + 1)
            pending.append([functools.partial(f, l + 1) for f in (sum1, sum2, sum3, sum4, sum5, sum6, sum7)])
        advance()
        halo_wait(l)
        shift(l)
        advance()
        if l:
            collect(top - l + 1, there)
            data(l, mine)
            advance()
    weight(0)
    pending.append([functools.partial(f, 0) for f in (sum1, sum2, sum3, sum4, sum5, sum6, sum7)])
    advance()
    data(0, gradient)
    while any(pending):
        advance()
    for t in range(layers):
        for j in range(chips):
            finish(first(t, j))
            for h in range(2):
                finish(second(t, j, h))


def per_device(cotangent, activations, active_masks, weights):
    height, extent, channels = cotangent.shape
    rows, cols = lax.axis_size("row"), lax.axis_size("col")
    chips = rows // 2
    layers = weights.shape[0]
    rim = 2 ** (layers - 1)
    lines = 9 * channels
    share = pl.cdiv(lines, rows * 16) * 16
    slab = pl.cdiv(share, cols * 16) * 16
    taps = weights.reshape(layers, 3, 3, channels, channels)
    straight = jnp.transpose(taps, (0, 1, 2, 4, 3))
    swapped = jnp.transpose(taps, (0, 2, 1, 4, 3))
    kernels = jnp.concatenate([straight, swapped], axis=-1)
    kernels = kernels.reshape(layers, 3, 3 * channels, 2 * channels)
    dma = pltpu.SemaphoreType.DMA
    gradient, total = pl.pallas_call(
        functools.partial(whole_kernel, layers, rows, cols, share, slab),
        out_shape=[
            jax.ShapeDtypeStruct((height, extent, channels), NARROW),
            jax.ShapeDtypeStruct((layers, rows * share, channels), NARROW),
        ],
        in_specs=[VMEM] * 4,
        out_specs=[VMEM] * 2,
        scratch_shapes=[
            pltpu.VMEM((layers - 1, height, extent, channels), NARROW),
            pltpu.VMEM((layers, chips, height // chips, extent, channels), NARROW),
            pltpu.VMEM((layers, extent, height, channels), NARROW),
            pltpu.VMEM((height, extent, channels), NARROW),
            pltpu.VMEM((height, extent, channels), NARROW),
            pltpu.VMEM((layers, height + 2 * rim, extent + 2 * EDGE, channels), NARROW),
            pltpu.VMEM((2, height + 2 * rim, extent, 3 * channels), NARROW),
            pltpu.VMEM((layers, rows * share, channels), WIDE),
            pltpu.VMEM((layers, chips * share, channels), WIDE),
            pltpu.VMEM((layers, chips * share, channels), NARROW),
            pltpu.VMEM((layers, chips, share, channels), NARROW),
            pltpu.VMEM((layers, cols * slab, channels), NARROW),
            pltpu.VMEM((layers, cols, slab, channels), NARROW),
            pltpu.VMEM((layers, cols * slab, channels), NARROW),
            dma((layers, chips)), dma((layers, chips)),
            dma((layers, rows)), dma((layers, rows)),
            dma((layers, 8)), dma((layers, 8)),
            dma((layers,)), dma((layers,)),
            dma((layers, chips)), dma((layers, chips)),
            dma((layers, cols)), dma((layers, cols)),
            dma((layers, cols)), dma((layers, cols)),
            dma((layers, chips)), dma((layers, chips)),
            dma((layers,)), dma((layers,)),
        ],
        compiler_params=pltpu.CompilerParams(
            collective_id=1, has_side_effects=True, vmem_limit_bytes=60 * 2**20
        ),
    )(cotangent, activations, active_masks, kernels)
    kernel_stack = total[:, :lines].reshape(weights.shape).astype(WIDE)
    return gradient, kernel_stack


def solution(mesh):
    in_specs = (
        P("row", "col", None),
        P(None, "row", "col", None),
        P(None, "row", "col", None),
        P(),
    )
    out_specs = (P("row", "col", None), P())
    return jax.shard_map(
        per_device, mesh=mesh, in_specs=in_specs, out_specs=out_specs, check_vma=False
    )
```

time: 378 us -> 124 us (0.33)
  blocking collectives: 168 us -> 0 us
  waiting for transfers between devices: 149 us -> 0 us
  Pallas kernels: 0 us -> 115 us
  starting transfers between devices: 18.2 us -> 0 us
  matrix products: 14.2 us -> 0 us
  between operations: 14.6 us -> 0.68 us
  local copies, waits for them, and re-layouts: 8.85 us -> 4.26 us
    all_to_all x9 -> x0, blocking collectives: 168 us -> none  [the longest x3 58.2 us: mirrored(): lax.all_to_all(local_tile, 'col', split_axis=0, concat_axis=1, tiled=True)]
    psum x1 -> x0, waiting for transfers between devices: 131 us -> none  [per_device(): collected.append(lax.psum(partial_value, ('row', 'col')))]
    pallas_call x0 -> x1, Pallas kernels: none -> 115 us  [per_device(): pl.pallas_call(functools.partial(whole_kernel, layers, rows, cols, share,...]
    ppermute x12 -> x0, waiting for transfers between devices: 18.7 us -> none  [the longest x6 18.5 us: extended(): lax.ppermute(lax.slice_in_dim(block, 0, width, axis=dim), axis, backward)]
    ppermute x12 -> x0, starting transfers between devices: 18.2 us -> none  [the longest x6 10.2 us: extended(): lax.ppermute(lax.slice_in_dim(block, block.shape[dim] - width, None, axis...]
    dot_general x6 -> x0, matrix products: 14.2 us -> none  [the longest x3 7.38 us: per_device(): jnp.einsum('yxko,kio->yxi', stacked, weights[layer_index], preferred_elem...]
    unnamed x29 -> x5, local copies, waits for them, and re-layouts: 6.55 us -> 0.8 us
  transfers between devices with their start and end apart: 13 -> 0, of which waited for: 8 -> 0; matrix products, arithmetic and copies ran while one was open for 3% -> 0% of each run, Pallas kernels for 0% -> 0%
where the time goes in v3:
time: 124 us
  Pallas kernels  115 us (93%)
  local copies, waits for them, and re-layouts  4.26 us (3%)
  other arithmetic  4.08 us (3%)
    pallas_call x1, Pallas kernels, per_device(): pl.pallas_call(functools.partial(whole_kernel, layers, rows, cols, share,...  115 us
    reshape x2, local copies, waits for them, and re-layouts, per_device(): taps = weights.reshape(layers, 3, 3, channels, channels)  3.46 us
    convert_element_type x1, other arithmetic, per_device(): kernel_stack = total[:, :lines].reshape(weights.shape).astype(WIDE)  2.64 us

profile of v3, /device:TPU:0, one launch (start us, length us, event | category | flops | bytes accessed | tf_op | source)
XLA Modules:
  0.0 123.6 jit_solution(16618991151731566340)
XLA Ops:
  0.6 0.0 copy-start
  0.6 2.1 %copy.7 = bf16[3,3,3,128,128]{3,4,1,2,0:T(8,128)(2,1)S(1)} copy(bf16[3,3,3,128,128]{4,3,2,1,0:T(8,128)(2,1)} %bitcast.9) | data formatting | bytes 1769472 | tf_op jit(solution)/shard_map/reshape | solution.py:360
  2.7 0.0 copy-done
  2.7 1.4 %copy.6 = bf16[3,3,3,128,128]{3,4,2,1,0:T(8,128)(2,1)S(1)} copy(bf16[3,3,3,128,128]{4,3,2,1,0:T(8,128)(2,1)S(1)} %bitcast.10) | data formatting | bytes 1769472 | tf_op jit(solution)/shard_map/reshape | solution.py:360
  4.1 1.4 %pad_maximum_fusion = bf16[3,3,3,128,256]{4,3,2,1,0:T(8,128)(2,1)} fusion(bf16[3,3,3,128,128]{4,3,2,1,0:T(8,128)(2,1)S(1)} %bitcast.7, bf16[3,3,3,128,128]{4,3,2,1,0:T(8,128)(2,1)S(1)} %bitcast.8), kind=kLoop, calls=%fused_computation | loop fusion | flops 3538944 | bytes 3538944 | tf_op jit(solution)/shard_map/concatenate | solution.py:363
  5.6 114.6 %shard_map.59 = (bf16[32,64,128]{2,1,0:T(8,128)(2,1)}, bf16[3,1152,128]{2,1,0:T(8,128)(2,1)}) custom-call(bf16[32,64,128]{2,1,0:T(8,128)(2,1)} %refs_0_.1, bf16[3,32,64,128]{3,2,1,0:T(8,128)(2,1)} %refs_1_.1, s32[3,32,64,128]{3,2,1,0:T(8,128)} %refs_2_.1, bf16[3,3,384,256]{3,2,1,0:T(8,128)(2,1)} %bitcast.6), custom_call_target="tpu_custom_call" | custom-call | tf_op jit(solution)/shard_map/pallas_call | solution.py:366
  120.1 0.0 copy-start.1
  120.2 2.6 %convert.1 = f32[3,9,128,128]{3,2,1,0:T(8,128)} convert(bf16[3,9,128,128]{3,2,1,0:T(8,128)(2,1)} %bitcast.11) | non-fusion elementwise | flops 442368 | bytes 2654208 | tf_op jit(solution)/shard_map/convert_element_type | solution.py:403
  122.8 0.0 copy-done.1
  122.8 0.8 copy.9
Async XLA Ops:
  0.6 2.1 %copy-start = (bf16[3,9,128,128]{3,2,1,0:T(8,128)(2,1)S(1)}, bf16[3,9,128,128]{3,2,1,0:T(8,128)(2,1)}, u32[]{:S(2)}) copy-start(bf16[3,9,128,128]{3,2,1,0:T(8,128)(2,1)} %param.7) | copy-start | bytes 2654212
  120.1 2.7 %copy-start.1 = (bf16[32,64,128]{2,1,0:T(8,128)(2,1)S(1)}, bf16[32,64,128]{2,1,0:T(8,128)(2,1)}, u32[]{:S(2)}) copy-start(bf16[32,64,128]{2,1,0:T(8,128)(2,1)} %get-tuple-element.8) | copy-start | bytes 1572868

commit v4 on v3

--- a/solution.py
+++ b/solution.py
@@ -184,19 +184,29 @@
         start = rim + 2**l * (1 - a) + n * CHUNK
         return shifted[l % 2, pl.ds(start, CHUNK)].reshape(CHUNK * extent, 3 * channels)
 
+    def against(value, weight):
+        return lax.dot_general(
+            value, weight, (((1,), (1,)), ((), ())), preferred_element_type=WIDE
+        )
+
     def data(l, mine):
         @pl.loop(0, height // CHUNK)
         def _(n):
             at = pl.ds(n * CHUNK, CHUNK)
-            change = jnp.zeros((CHUNK * extent, (2 if l else 1) * channels), WIDE)
+            own = jnp.zeros((CHUNK * extent, channels), WIDE)
+            flipped = own
             for a in range(3):
-                weight = kernels[l, a] if l else kernels[l, a, :, :channels]
-                change += jnp.dot(cells(l, a, n), weight, preferred_element_type=WIDE)
-            own = change[:, :channels].reshape(CHUNK, extent, channels)
+                values = cells(l, a, n)
+                for b in range(3):
+                    value = values[:, b * channels : (b + 1) * channels]
+                    own += against(value, kernels[l, 3 * a + b])
+                    if l:
+                        flipped += against(value, kernels[l, 3 * b + a])
+            own = own.reshape(CHUNK, extent, channels)
             new = mine[at].astype(WIDE) + jnp.where(masks[l, at] > 0, own, 0.0)
             gradient[at] = new.astype(NARROW)
             if l:
-                own = change[:, channels:].reshape(CHUNK, extent, channels)
+                own = flipped.reshape(CHUNK, extent, channels)
                 open_ = there[at].astype(WIDE) > 0
                 new = opposite[at].astype(WIDE) + jnp.where(open_, own, 0.0)
                 opposite[at] = new.astype(NARROW)
@@ -308,11 +318,12 @@
     for t in range(layers):
         for j in range(chips):
             begin(first(t, j))
-    forward(0)
-    for t in range(1, layers):
-        forward(t)
+        if t:
+            forward(t - 1)
+    forward(layers - 1)
     collect(0, opposite)
     pending = []
+    SUMS = (sum1, sum2, sum3, sum4, sum5, sum6, sum7)
 
     def advance():
         for steps in pending:
@@ -324,21 +335,17 @@
         mine = cotangent if l == top else gradient
         symmetrize(l, mine)
         halo_start(l)
-        if l < top:
-            weight(l + 1)
-            pending.append([functools.partial(f, l + 1) for f in (sum1, sum2, sum3, sum4, sum5, sum6, sum7)])
         advance()
         halo_wait(l)
         shift(l)
+        weight(l)
+        pending.append([functools.partial(f, l) for f in SUMS])
         advance()
         if l:
             collect(top - l + 1, there)
-            data(l, mine)
+        data(l, mine)
+        if l:
             advance()
-    weight(0)
-    pending.append([functools.partial(f, 0) for f in (sum1, sum2, sum3, sum4, sum5, sum6, sum7)])
-    advance()
-    data(0, gradient)
     while any(pending):
         advance()
     for t in range(layers):
@@ -357,11 +364,6 @@
     lines = 9 * channels
     share = pl.cdiv(lines, rows * 16) * 16
     slab = pl.cdiv(share, cols * 16) * 16
-    taps = weights.reshape(layers, 3, 3, channels, channels)
-    straight = jnp.transpose(taps, (0, 1, 2, 4, 3))
-    swapped = jnp.transpose(taps, (0, 2, 1, 4, 3))
-    kernels = jnp.concatenate([straight, swapped], axis=-1)
-    kernels = kernels.reshape(layers, 3, 3 * channels, 2 * channels)
     dma = pltpu.SemaphoreType.DMA
     gradient, total = pl.pallas_call(
         functools.partial(whole_kernel, layers, rows, cols, share, slab),
@@ -399,7 +401,7 @@
         compiler_params=pltpu.CompilerParams(
             collective_id=1, has_side_effects=True, vmem_limit_bytes=60 * 2**20
         ),
-    )(cotangent, activations, active_masks, kernels)
+    )(cotangent, activations, active_masks, weights)
     kernel_stack = total[:, :lines].reshape(weights.shape).astype(WIDE)
     return gradient, kernel_stack
 

time: 124 us -> 120 us (0.968)
  local copies, waits for them, and re-layouts: 4.26 us -> 0.8 us
  other arithmetic: 4.08 us -> 2.64 us
    reshape x2 -> x0, local copies, waits for them, and re-layouts: 3.46 us -> none  [per_device(): taps = weights.reshape(layers, 3, 3, channels, channels)]
    concatenate x1 -> x0, other arithmetic: 1.44 us -> none  [per_device(): kernels = jnp.concatenate([straight, swapped], axis=-1)]
where the time goes in v4:
time: 120 us
  Pallas kernels  116 us (97%)
  other arithmetic  2.64 us (2%)
    pallas_call x1, Pallas kernels, per_device(): pl.pallas_call(functools.partial(whole_kernel, layers, rows, cols, share,...  116 us
    convert_element_type x1, other arithmetic, per_device(): kernel_stack = total[:, :lines].reshape(weights.shape).astype(WIDE)  2.64 us

profile of v4, /device:TPU:0, one launch (start us, length us, event | category | flops | bytes accessed | tf_op | source)
XLA Modules:
  0.0 119.9 jit_solution(7328944390580959925)
XLA Ops:
  0.6 115.8 %shard_map.59 = (bf16[32,64,128]{2,1,0:T(8,128)(2,1)}, bf16[3,1152,128]{2,1,0:T(8,128)(2,1)}) custom-call(bf16[32,64,128]{2,1,0:T(8,128)(2,1)} %refs_0_.1, bf16[3,32,64,128]{3,2,1,0:T(8,128)(2,1)} %refs_1_.1, s32[3,32,64,128]{3,2,1,0:T(8,128)} %refs_2_.1, bf16[3,9,128,128]{3,2,1,0:T(8,128)(2,1)} %refs_3_.1), custom_call_target="tpu_custom_call" | custom-call | tf_op jit(solution)/shard_map/pallas_call | solution.py:368
  116.4 0.0 copy-start
  116.4 2.6 %convert.1 = f32[3,9,128,128]{3,2,1,0:T(8,128)} convert(bf16[3,9,128,128]{3,2,1,0:T(8,128)(2,1)} %bitcast.2) | non-fusion elementwise | flops 442368 | bytes 2654208 | tf_op jit(solution)/shard_map/convert_element_type | solution.py:405
  119.1 0.0 copy-done
  119.1 0.8 copy.7
Async XLA Ops:
  116.4 2.7 %copy-start = (bf16[32,64,128]{2,1,0:T(8,128)(2,1)S(1)}, bf16[32,64,128]{2,1,0:T(8,128)(2,1)}, u32[]{:S(2)}) copy-start(bf16[32,64,128]{2,1,0:T(8,128)(2,1)} %get-tuple-element.8) | copy-start | bytes 1572868
